TPU v7x, 32 devices: a whole 2x2x4 slice. The times are simulated.
32 devices in a mesh: mem: 4 (over y, x), strip: 8 (over z, core).
Axes of the slice: x: 2, y: 2, z: 4, core: 2. Of those that a mesh axis runs over, the one named last changes fastest.
Arguments:
- ensemble: float32 [256, 64, 256], P('mem', 'strip'), may hold values from -12 to 12
- forcing: float32 [64, 256], P('strip'), may hold values from 4 to 12
- obs_index: int32 [64, 128], P(('strip', 'mem')), may hold values from 0 to 255
- obs_count: int32 [64], P(('strip', 'mem')), may hold values from 1 to 128, as said below
- obs_value: float32 [64, 128], P(('strip', 'mem')), may hold values from -18 to 18
- obs_precision: float32 [64, 128], P(('strip', 'mem')), may hold values from 0.05 to 1
Outputs:
- analysis: float32 [256, 64, 256], P('mem', 'strip')
Inputs may be any that keep to these rules, and one draw needn't show every extreme that they name: The live observations of a region are the first obs_count of its slots; in every draw some region has all 128 slots live. `obs_index`: position of the observed cell within its region; a cell may be observed more than once.
All inputs are finite; a program needn't handle non-finite values.
Results may differ from a plain program's by a relative error of at most 0.0003.
Values sent between devices are 32-bit elements; how exact they have to be, the bound alone decides.
A program may use at most 64 MiB of HBM per device.

v0:
```python
import math

import jax
import jax.numpy as jnp
from jax import lax
from jax.sharding import PartitionSpec as P

STEPS = 4
NS_ITERS = 4
REGION_VALUES = 256


step_size = 0.05
coupling = 0.4


def padded(block, sides, width):
    for axis, dim in sides:
        count = lax.axis_size(axis)
        forward = [(i, i + 1) for i in range(count - 1)]
        backward = [(target, source) for source, target in forward]
        low = lax.ppermute(
            lax.slice_in_dim(block, block.shape[dim] - width, None, axis=dim), axis, forward
        )
        high = lax.ppermute(lax.slice_in_dim(block, 0, width, axis=dim), axis, backward)
        block = jnp.concatenate([low, block, high], axis=dim)
    return block


def march_forward(padded_state, forcing_rows):
    center = padded_state[:, 1:-1]
    meridional = padded_state[:, 2:] + padded_state[:, :-2] - 2.0 * center
    advection = (jnp.roll(center, -1, 2) - jnp.roll(center, 2, 2)) * jnp.roll(center, 1, 2)
    return center + step_size * (advection - center + forcing_rows) + coupling * meridional


def analyze(members, obs_index, obs_count, obs_value, obs_precision):
    highest = lax.Precision.HIGHEST
    ens_size = members.shape[0]
    member_mean = jnp.mean(members, axis=0)
    spread = members - member_mean[None]
    cell_ids = jnp.arange(members.shape[2], dtype=jnp.int32)
    onehot = (obs_index[:, :, None] == cell_ids[None, None, :]).astype(jnp.float32)
    slot_ids = jnp.arange(obs_index.shape[1], dtype=jnp.int32)
    live_mask = (slot_ids[None, :] < obs_count[:, None]).astype(jnp.float32)
    obs_spread = jnp.einsum("roc,krc->rok", onehot, spread, precision=highest)
    obs_mean = jnp.einsum("roc,rc->ro", onehot, member_mean, precision=highest)
    weight = obs_precision * live_mask
    innovation = weight * (obs_value - obs_mean)
    gram_matrix = jnp.einsum(
        "roj,rok->rjk", obs_spread * weight[:, :, None], obs_spread, precision=highest
    )
    identity = jnp.eye(ens_size, dtype=jnp.float32)
    norm_scale = ens_size - 1.0 + jnp.sqrt(jnp.sum(gram_matrix * gram_matrix, axis=(1, 2)))
    left_iterate = ((ens_size - 1.0) * identity + gram_matrix) / norm_scale[:, None, None]
    right_iterate = jnp.broadcast_to(identity, gram_matrix.shape)
    for repeat in range(NS_ITERS):
        correction = 1.5 * identity - 0.5 * jnp.einsum(
            "rij,rjk->rik", right_iterate, left_iterate, precision=highest
        )
        left_iterate = jnp.einsum("rij,rjk->rik", left_iterate, correction, precision=highest)
        right_iterate = jnp.einsum("rij,rjk->rik", correction, right_iterate, precision=highest)
    inv_root = right_iterate / jnp.sqrt(norm_scale)[:, None, None]
    projected = jnp.einsum("roj,ro->rj", obs_spread, innovation, precision=highest)
    halfway = jnp.einsum("rjk,rk->rj", inv_root, projected, precision=highest)
    mean_weights = jnp.einsum("rjk,rk->rj", inv_root, halfway, precision=highest)
    transform = math.sqrt(ens_size - 1.0) * inv_root + mean_weights[:, :, None]
    return member_mean[None] + jnp.einsum("rjk,jrc->krc", transform, spread, precision=highest)


def local(ensemble, forcing, obs_index, obs_count, obs_value, obs_precision):
    regional_members, latitude_rows, longitude_cells = ensemble.shape
    stacked = jnp.concatenate([ensemble, forcing[None]], axis=0)
    padded_state = padded(stacked, (("strip", 1),), STEPS)
    forcing_pad = padded_state[regional_members]
    current = padded_state[:regional_members]
    strip_id = lax.axis_index("strip")
    global_rows = strip_id * latitude_rows + jnp.arange(
        -STEPS, latitude_rows + STEPS, dtype=jnp.int32
    )
    inside = ((global_rows >= 0) & (global_rows < latitude_rows * lax.axis_size("strip"))).astype(
        jnp.float32
    )
    for sweep_index in range(STEPS):
        rows_next = current.shape[1] - 2
        advanced = march_forward(
            current, forcing_pad[sweep_index + 1 : sweep_index + 1 + rows_next]
        )
        current = advanced * inside[sweep_index + 1 : sweep_index + 1 + rows_next][None, :, None]
    flat_state = current.reshape(regional_members, latitude_rows * longitude_cells)
    mem_count = lax.axis_size("mem")
    region_cells = latitude_rows * longitude_cells // mem_count
    regional = lax.all_to_all(flat_state, "mem", split_axis=1, concat_axis=0, tiled=True)
    blocks = regional.reshape(regional.shape[0], region_cells // REGION_VALUES, REGION_VALUES)
    analysis = analyze(blocks, obs_index, obs_count, obs_value, obs_precision)
    analysis = analysis.reshape(regional.shape[0], region_cells)
    members_back = lax.all_to_all(analysis, "mem", split_axis=0, concat_axis=1, tiled=True)
    return members_back.reshape(regional_members, latitude_rows, longitude_cells)


def solution(mesh):
    placed = (
        P("mem", "strip", None),
        P("strip", None),
        P(("strip", "mem"), None),
        P(("strip", "mem")),
        P(("strip", "mem"), None),
        P(("strip", "mem"), None),
    )
    return jax.shard_map(
        local, mesh=mesh, in_specs=placed, out_specs=P("mem", "strip", None), check_vma=False
    )
```

profile of v0, /device:TPU:17, one launch (start us, length us, event | category | flops | bytes accessed | tf_op | source)
XLA Modules:
  0.0 57.9 jit_solution(8702646043264402413)
XLA Ops:
  0.0 1.4 %fusion.45 = (f32[65,4,256]{2,1,0:T(4,128)S(1)}, f32[65,4,256]{2,1,0:T(4,128)S(1)}) fusion(f32[64,8,256]{2,1,0:T(8,128)} %param.6, f32[1,8,256]{2,1,0:T(8,128)} %bitcast.61), kind=kLoop, calls=%fused_computation.64 | loop fusion | flops 133120 | bytes 1064960 | tf_op jit(solution)/shard_map/concatenate | solution.py:73
  1.5 3.9 %collective-permute-start = (f32[65,4,256]{2,0,1:T(8,128)S(1)}, f32[65,4,256]{2,0,1:T(8,128)S(1)}, u32[]{:S(2)}, u32[]{:S(2)}) collective-permute-start(f32[65,4,256]{2,0,1:T(8,128)S(1)} %copy.38), channel_id=1, source_target_pairs={{0,1},{1,2},{2,3},{3,4},{4,5},{5,6},{6,7},{8,9},{9,10},{10,11},{11... | collective-permute-start | bytes 798728 | tf_op jit(solution)/shard_map/ppermute | solution.py:22
  5.5 1.9 %collective-permute-start.1 = (f32[65,4,256]{2,0,1:T(8,128)S(1)}, f32[65,4,256]{2,0,1:T(8,128)S(1)}, u32[]{:S(2)}, u32[]{:S(2)}) collective-permute-start(f32[65,4,256]{2,0,1:T(8,128)S(1)} %copy.39), channel_id=1, source_target_pairs={{1,0},{2,1},{3,2},{4,3},{5,4},{6,5},{7,6},{9,8},{10,9},{11,10},{12... | collective-permute-start | bytes 798728 | tf_op jit(solution)/shard_map/ppermute | solution.py:25
  7.7 1.3 %collective-permute-done = f32[65,4,256]{2,0,1:T(8,128)S(1)} collective-permute-done((f32[65,4,256]{2,0,1:T(8,128)S(1)}, f32[65,4,256]{2,0,1:T(8,128)S(1)}, u32[]{:S(2)}, u32[]{:S(2)}) %collective-permute-start) | collective-permute-done | bytes 266272 | tf_op jit(solution)/shard_map/ppermute | solution.py:22
  9.2 4.4 %collective-permute-done.1 = f32[65,4,256]{2,0,1:T(8,128)S(1)} collective-permute-done((f32[65,4,256]{2,0,1:T(8,128)S(1)}, f32[65,4,256]{2,0,1:T(8,128)S(1)}, u32[]{:S(2)}, u32[]{:S(2)}) %collective-permute-start.1) | collective-permute-done | bytes 266272 | tf_op jit(solution)/shard_map/ppermute | solution.py:25
  14.8 1.1 %fusion.16 = f32[64,14,256]{2,1,0:T(8,128)S(1)} fusion(f32[65,16,256]{2,1,0:T(8,128)S(1)} %pad_maximum_fusion, f32[64,14,1]{2,1,0:T(8,128)S(1)} %get-tuple-element.8, f32[64,14,255]{2,1,0:T(8,128)S(1)} %get-tuple-element.10, f32[64,14,254]{2,1,0:T(8,128)S(1)} %slice.249, f32[64,14,2]{2,1,0:T(8,128)S(1)} %slice.248, f32[64,14,255]{2,1,0:T(8,128)S(1)} %get-tuple-element.9, ...), kind=kLoop, calls=%fused_computation.26 | loop fusion | flops 3440640 | bytes 6436920 | tf_op jit(solution)/shard_map/mul | solution.py:89
  16.8 1.1 %fusion.12 = f32[64,12,256]{2,1,0:T(8,128)S(1)} fusion(f32[64,14,256]{2,1,0:T(8,128)S(1)} %fusion.16, f32[64,12,1]{2,1,0:T(8,128)S(1)} %get-tuple-element.20, f32[64,12,255]{2,1,0:T(8,128)S(1)} %get-tuple-element.22, f32[64,12,254]{2,1,0:T(8,128)S(1)} %slice.258, f32[64,12,2]{2,1,0:T(8,128)S(1)} %slice.257, f32[64,12,255]{2,1,0:T(8,128)S(1)} %get-tuple-element.21, ...), kind=kLoop, calls=%fused_computation.21 | loop fusion | flops 2949120 | bytes 5517360 | tf_op jit(solution)/shard_map/mul | solution.py:89
  18.9 1.1 %fusion.8 = f32[64,10,256]{2,1,0:T(8,128)S(1)} fusion(f32[64,12,256]{2,1,0:T(8,128)S(1)} %fusion.12, f32[64,10,1]{2,1,0:T(8,128)S(1)} %get-tuple-element.16, f32[64,10,255]{2,1,0:T(8,128)S(1)} %get-tuple-element.18, f32[64,10,254]{2,1,0:T(8,128)S(1)} %slice.267, f32[64,10,2]{2,1,0:T(8,128)S(1)} %slice.266, f32[64,10,255]{2,1,0:T(8,128)S(1)} %get-tuple-element.17, ...), kind=kLoop, calls=%fused_computation.16 | loop fusion | flops 2457600 | bytes 4597800 | tf_op jit(solution)/shard_map/mul | solution.py:89
  21.2 1.0 %copy.42 = f32[64,4,512]{2,0,1:T(8,128)} copy(f32[64,4,512]{2,1,0:T(4,128)S(1)} %all_to_all.24) | data formatting | bytes 1048576 | tf_op jit(solution)/shard_map/all_to_all | solution.py:93
  22.2 3.7 %all-to-all-start = ((f32[64,4,512]{2,0,1:T(8,128)}), f32[64,4,512]{2,0,1:T(8,128)S(1)}, u32[]{:S(2)}, u32[]{:S(2)}) async-start(f32[64,4,512]{2,0,1:T(8,128)} %copy.42), calls=%async_computation | async-start | bytes 1048576 | tf_op jit(solution)/shard_map/all_to_all | solution.py:93
  25.9 7.4 %all-to-all-done = f32[64,4,512]{2,0,1:T(8,128)S(1)} async-done(((f32[64,4,512]{2,0,1:T(8,128)}), f32[64,4,512]{2,0,1:T(8,128)S(1)}, u32[]{:S(2)}, u32[]{:S(2)}) %all-to-all-start) | async-done | bytes 524320 | tf_op jit(solution)/shard_map/all_to_all | solution.py:93
  35.1 0.8 %multiply_reduce_fusion = (f32[2]{0:T(128)S(1)}, f32[2,256,256]{2,1,0:T(8,128)S(1)}) fusion(f32[2,128,256]{2,1,0:T(8,128)S(1)} %fusion.49, f32[2,128]{1,0:T(2,128)S(1)} %get-tuple-element.6), kind=kOutput, calls=%fused_computation.60 | convolution fusion | flops 201654272 | bytes 787464 | tf_op jit(solution)/shard_map/roj,rok->rjk/dot_general | solution.py:50
  35.9 0.7 %fusion.4 = f32[2,256,256]{2,1,0:T(8,128)S(1)} fusion(f32[256,256]{1,0:T(8,128)S(1)} %fusion.54, f32[256,256]{1,0:T(8,128)S(1)} %get-tuple-element.30, f32[2,256,256]{2,1,0:T(8,128)S(1)} %get-tuple-element.28, f32[2]{0:T(128)S(1)} %get-tuple-element.26, f32[256,256]{1,0:T(8,128)S(1)} %get-tuple-element.29), kind=kOutput, calls=%fused_computation.10 | convolution fusion | flops 403177472 | bytes 1835016 | tf_op jit(solution)/shard_map/rij,rjk->rik/dot_general | solution.py:58
  36.7 0.7 %fusion.65 = f32[2,256,256]{2,1,0:T(8,128)S(1)} fusion(f32[2,256,256]{2,1,0:T(8,128)S(1)} %fusion.4, f32[2,256,256]{2,1,0:T(8,128)S(1)} %get-tuple-element.28, f32[2]{0:T(128)S(1)} %get-tuple-element.26, f32[256,256]{1,0:T(8,128)S(1)} %get-tuple-element.29), kind=kOutput, calls=%fused_computation.99 | convolution fusion | flops 402915328 | bytes 1835016 | tf_op jit(solution)/shard_map/rij,rjk->rik/dot_general | solution.py:61
  38.0 0.7 %fusion.3 = f32[2,256,256]{2,1,0:T(8,128)S(1)} fusion(f32[2,256,256]{2,1,0:T(8,128)S(1)} %fusion.50, f32[2,256,256]{2,1,0:T(8,128)S(1)} %fusion.65, f32[256,256]{1,0:T(8,128)S(1)} %get-tuple-element.30), kind=kOutput, calls=%fused_computation.8 | convolution fusion | flops 402915328 | bytes 1835008 | tf_op jit(solution)/shard_map/rij,rjk->rik/dot_general | solution.py:58
  38.7 0.7 %fusion.75 = f32[2,256,256]{2,1,0:T(8,128)S(1)} fusion(f32[2,256,256]{2,1,0:T(8,128)S(1)} %fusion.65, f32[2,256,256]{2,1,0:T(8,128)S(1)} %fusion.3), kind=kOutput, calls=%fused_computation.109 | convolution fusion | flops 402653184 | bytes 1572864 | tf_op jit(solution)/shard_map/rij,rjk->rik/dot_general | solution.py:61
  39.3 0.7 %fusion.74 = f32[2,256,256]{2,1,0:T(8,128)S(1)} fusion(f32[2,256,256]{2,1,0:T(8,128)S(1)} %fusion.3, f32[2,256,256]{2,1,0:T(8,128)S(1)} %fusion.50), kind=kOutput, calls=%fused_computation.108 | convolution fusion | flops 402653184 | bytes 1572864 | tf_op jit(solution)/shard_map/rij,rjk->rik/dot_general | solution.py:62
  40.0 0.7 %fusion.2 = f32[2,256,256]{2,1,0:T(8,128)S(1)} fusion(f32[2,256,256]{2,1,0:T(8,128)S(1)} %fusion.74, f32[2,256,256]{2,1,0:T(8,128)S(1)} %fusion.75, f32[256,256]{1,0:T(8,128)S(1)} %get-tuple-element.30), kind=kOutput, calls=%fused_computation.6 | convolution fusion | flops 402915328 | bytes 1835008 | tf_op jit(solution)/shard_map/rij,rjk->rik/dot_general | solution.py:58
  40.7 0.7 %fusion.77 = f32[2,256,256]{2,1,0:T(8,128)S(1)} fusion(f32[2,256,256]{2,1,0:T(8,128)S(1)} %fusion.75, f32[2,256,256]{2,1,0:T(8,128)S(1)} %fusion.2), kind=kOutput, calls=%fused_computation.111 | convolution fusion | flops 402653184 | bytes 1572864 | tf_op jit(solution)/shard_map/rij,rjk->rik/dot_general | solution.py:61
  42.2 0.7 %fusion.1 = f32[2,256,256]{2,1,0:T(8,128)S(1)} fusion(f32[2,256,256]{2,1,0:T(8,128)S(1)} %fusion.76, f32[2,256,256]{2,1,0:T(8,128)S(1)} %fusion.77, f32[256,256]{1,0:T(8,128)S(1)} %get-tuple-element.30), kind=kOutput, calls=%fused_computation.4 | convolution fusion | flops 402915328 | bytes 1835008 | tf_op jit(solution)/shard_map/rij,rjk->rik/dot_general | solution.py:58
  42.9 0.7 %convolution_divide_fusion = f32[2,256,256]{2,1,0:T(8,128)S(1)} fusion(f32[2,256,256]{2,1,0:T(8,128)S(1)} %fusion.1, f32[2,256,256]{2,1,0:T(8,128)S(1)} %fusion.76, f32[2]{0:T(128)S(1)} %get-tuple-element.25), kind=kOutput, calls=%fused_computation.2 | convolution fusion | flops 402784256 | bytes 1572872 | tf_op jit(solution)/shard_map/rij,rjk->rik/dot_general | solution.py:62
  44.7 0.8 %fusion = f32[256,2,256]{0,2,1:T(8,128)S(1)} fusion(f32[256,2,256]{0,2,1:T(8,128)S(1)} %copy.45, f32[2,256,256]{2,1,0:T(8,128)S(1)} %convolution_divide_fusion, f32[2,256]{1,0:T(2,128)S(1)} %bitcast.68, f32[2,256]{1,0:T(2,128)S(1)} %div.26), kind=kOutput, calls=%fused_computation.1 | convolution fusion | flops 403046400 | bytes 1576960 | tf_op jit(solution)/shard_map/rjk,jrc->krc/dot_general | solution.py:68
  46.1 10.4 %all_to_all.32 = f32[4,64,512]{2,1,0:T(8,128)S(1)} all-to-all(f32[4,64,512]{2,1,0:T(8,128)S(1)} %all_to_all.27), channel_id=1, replica_groups=mesh['mem'=4,'strip'=8] {'mem'}, dimensions={0} | all-to-all | bytes 1048576 | tf_op jit(solution)/shard_map/all_to_all | solution.py:97
  56.9 1.0 %reshape.65 = f32[64,8,256]{2,1,0:T(8,128)} reshape(f32[64,4,512]{2,1,0:T(4,128)S(1)} %copy.47) | data formatting | bytes 1048576 | tf_op jit(solution)/shard_map/reshape | solution.py:98
  (67 shorter events, 10.3 us)
Async XLA Ops:
  1.4 12.2 %copy-start = (f32[64,8,256]{2,1,0:T(8,128)S(1)}, f32[64,8,256]{2,1,0:T(8,128)}, u32[]{:S(2)}) copy-start(f32[64,8,256]{2,1,0:T(8,128)} %param.6) | copy-start | bytes 1572868
  1.4 12.2 %copy-start.1 = (f32[8,256]{1,0:T(8,128)S(1)}, f32[8,256]{1,0:T(8,128)}, u32[]{:S(2)}) copy-start(f32[8,256]{1,0:T(8,128)} %param.7) | copy-start | bytes 24580
  1.5 7.6 %collective-permute-start = (f32[65,4,256]{2,0,1:T(8,128)S(1)}, f32[65,4,256]{2,0,1:T(8,128)S(1)}, u32[]{:S(2)}, u32[]{:S(2)}) collective-permute-start(f32[65,4,256]{2,0,1:T(8,128)S(1)} %copy.38), channel_id=1, source_target_pairs={{0,1},{1,2},{2,3},{3,4},{4,5},{5,6},{6,7},{8,9},{9,10},{10,11},{11... | collective-permute-start | bytes 798728 | tf_op jit(solution)/shard_map/ppermute | solution.py:22
  5.5 8.0 %collective-permute-start.1 = (f32[65,4,256]{2,0,1:T(8,128)S(1)}, f32[65,4,256]{2,0,1:T(8,128)S(1)}, u32[]{:S(2)}, u32[]{:S(2)}) collective-permute-start(f32[65,4,256]{2,0,1:T(8,128)S(1)} %copy.39), channel_id=1, source_target_pairs={{1,0},{2,1},{3,2},{4,3},{5,4},{6,5},{7,6},{9,8},{10,9},{11,10},{12... | collective-permute-start | bytes 798728 | tf_op jit(solution)/shard_map/ppermute | solution.py:25
  22.2 11.1 %all-to-all-start = ((f32[64,4,512]{2,0,1:T(8,128)}), f32[64,4,512]{2,0,1:T(8,128)S(1)}, u32[]{:S(2)}, u32[]{:S(2)}) async-start(f32[64,4,512]{2,0,1:T(8,128)} %copy.42), calls=%async_computation | async-start | bytes 1048576 | tf_op jit(solution)/shard_map/all_to_all | solution.py:93
  33.7 0.7 %copy-start.2 = (s32[2,128]{1,0:T(2,128)S(1)}, s32[2,128]{1,0:T(2,128)}, u32[]{:S(2)}) copy-start(s32[2,128]{1,0:T(2,128)} %param.8) | copy-start | bytes 3076
  33.8 1.2 %copy-start.3 = (f32[2,128]{1,0:T(2,128)S(1)}, f32[2,128]{1,0:T(2,128)}, u32[]{:S(2)}) copy-start(f32[2,128]{1,0:T(2,128)} %param.10) | copy-start | bytes 3076
  33.8 1.2 %copy-start.4 = (f32[2,128]{1,0:T(2,128)S(1)}, f32[2,128]{1,0:T(2,128)}, u32[]{:S(2)}) copy-start(f32[2,128]{1,0:T(2,128)} %param.11) | copy-start | bytes 3076
  33.8 1.2 %copy-start.5 = (s32[2]{0:T(128)S(1)}, s32[2]{0:T(128)}, u32[]{:S(2)}) copy-start(s32[2]{0:T(128)} %param.9) | copy-start | bytes 28
where the time goes:
time: 59 us; the launch traced here: 57.9 us
  waiting for transfers between devices  13.1 us (22%)
  matrix products  10.8 us (18%)
  blocking collectives  10.4 us (18%)
  starting transfers between devices  9.47 us (16%)
  local copies, waits for them, and re-layouts  8.07 us (14%)
  other arithmetic  5.56 us (9%)
    all_to_all x1, blocking collectives, local(): lax.all_to_all(analysis, 'mem', split_axis=0, concat_axis=1, tiled=True)  10.4 us
    all_to_all x1, waiting for transfers between devices, local(): lax.all_to_all(flat_state, 'mem', split_axis=1, concat_axis=0, tiled=True)  7.39 us
    ppermute x1, waiting for transfers between devices, padded(): lax.ppermute(lax.slice_in_dim(block, 0, width, axis=dim), axis, backward)  4.35 us
    ppermute x1, starting transfers between devices, padded(): lax.ppermute(lax.slice_in_dim(block, block.shape[dim] - width, None, axis...  3.9 us
    mul x4, other arithmetic, local(): advanced * inside[sweep_index + 1:sweep_index + 1 + rows_next][None, :, N...  3.67 us
    all_to_all x1, starting transfers between devices, local(): lax.all_to_all(flat_state, 'mem', split_axis=1, concat_axis=0, tiled=True)  3.65 us
    dot_general x4, matrix products, analyze(): jnp.einsum('rij,rjk->rik', right_iterate, left_iterate, precision=highest)  2.7 us
    dot_general x4, matrix products, analyze(): jnp.einsum('rij,rjk->rik', correction, right_iterate, precision=highest)  2.59 us
  transfers between devices with their start and end apart: 3, of which 3 were waited for; matrix products, arithmetic and copies ran while one was open for 1% of the time, Pallas kernels for 0%

commit v1 on v0

v1 whole, which is shorter than its diff:
```python
import functools
import math

import jax
import jax.numpy as jnp
from jax import lax
from jax.experimental import pallas as pl
from jax.experimental.pallas import tpu as pltpu
from jax.sharding import PartitionSpec as P

STEPS = 4
NS_ITERS = 4
REGION_VALUES = 256
TILE = 8

step_size = 0.05
coupling = 0.4

MESH = pl.DeviceIdType.MESH
bf16 = jnp.bfloat16
f32 = jnp.float32


def split(x):
    hi = x.astype(bf16)
    lo = (x - hi.astype(f32)).astype(bf16)
    return hi, lo


def dot(a, b):
    return lax.dot_general(a, b, (((1,), (0,)), ((), ())), preferred_element_type=f32)


def wide_lhs(x):
    return jnp.concatenate(split(x), axis=1)


def small_rhs(x):
    both = jnp.concatenate(split(x), axis=1)
    return jnp.concatenate([both, both], axis=0)


def small_dot(lhs_parts, rhs):
    size = rhs.shape[0]
    lhs = jnp.concatenate([wide_lhs(part) for part in lhs_parts], axis=0)
    both = dot(lhs, small_rhs(rhs))
    total = both[:, :size] + both[:, size:]
    return [total[size * k : size * (k + 1)] for k in range(len(lhs_parts))]


def kernel(
    n_mem,
    n_strip,
    members,
    count_ref,
    x_ref,
    index_ref,
    value_ref,
    prec_ref,
    out_ref,
    halo,
    fc,
    rbuf,
    ana,
    bt_ref,
    e_ref,
    hsend,
    hrecv,
    asend,
    arecv,
    bsend,
    brecv,
):
    rows, padded_members, lon = x_ref.shape
    groups, obs = index_ref.shape
    chunks = asend.shape[0]
    per_chunk = members // chunks
    total = members * n_mem
    me = lax.axis_index("mem")
    strip = lax.axis_index("strip")
    has_low = strip > 0
    has_high = strip < n_strip - 1

    def place(owner, i):
        flat = (owner * groups + i) * REGION_VALUES
        return flat // lon, pl.multiple_of(flat % lon, REGION_VALUES)

    barrier = pltpu.get_barrier_semaphore()
    for d in range(1, n_mem):
        pl.semaphore_signal(
            barrier, inc=1, device_id=(lax.rem(me + d, n_mem), strip), device_id_type=MESH
        )

    @pl.when(has_low)
    def _():
        pl.semaphore_signal(barrier, inc=1, device_id=(me, strip - 1), device_id_type=MESH)

    @pl.when(has_high)
    def _():
        pl.semaphore_signal(barrier, inc=1, device_id=(me, strip + 1), device_id_type=MESH)

    pl.semaphore_wait(
        barrier, n_mem - 1 + jnp.where(has_low, 1, 0) + jnp.where(has_high, 1, 0)
    )

    def halo_copy(side):
        return pltpu.make_async_remote_copy(
            src_ref=x_ref.at[pl.ds(rows - STEPS if side == 0 else 0, STEPS)],
            dst_ref=halo.at[side],
            send_sem=hsend.at[side],
            recv_sem=hrecv.at[side],
            device_id=(me, strip + 1 if side == 0 else strip - 1),
            device_id_type=MESH,
        )

    sends = (has_high, has_low)
    receives = (has_low, has_high)
    for side in range(2):

        @pl.when(sends[side])
        def _(side=side):
            halo_copy(side).start()

        @pl.when(jnp.logical_not(receives[side]))
        def _(side=side):
            halo[side] = jnp.zeros(halo.shape[1:], f32)

    for side in range(2):

        @pl.when(receives[side])
        def _(side=side):
            halo_copy(side).wait_recv()

    low_in = jnp.where(has_low, 1.0, 0.0).astype(f32)
    high_in = jnp.where(has_high, 1.0, 0.0).astype(f32)

    def stacked(r, at):
        if r < STEPS:
            return halo[0, r, at, :]
        if r < STEPS + rows:
            return x_ref[r - STEPS, at, :]
        return halo[1, r - STEPS - rows, at, :]

    def march(tile):
        at = pl.ds(pl.multiple_of(tile * TILE, TILE), TILE)
        force_at = pl.ds(members, TILE)
        state = [stacked(r, at) for r in range(rows + 2 * STEPS)]
        first = 0
        for _ in range(STEPS):
            following = []
            for k in range(1, len(state) - 1):
                r = first + k
                u = state[k]
                advection = (pltpu.roll(u, lon - 1, 1) - pltpu.roll(u, 2, 1)) * pltpu.roll(u, 1, 1)
                new = (
                    (1.0 - step_size - 2.0 * coupling) * u
                    + step_size * (advection + stacked(r, force_at))
                    + coupling * (state[k - 1] + state[k + 1])
                )
                if r < STEPS:
                    new = new * low_in
                elif r >= STEPS + rows:
                    new = new * high_in
                following.append(new)
            state = following
            first += 1
        for r in range(rows):
            fc[r, at, :] = state[r]

    def out_copy(c, d, i):
        peer = lax.rem(me + d, n_mem)
        row, col = place(peer, i)
        at = pl.ds(c * per_chunk, per_chunk)
        return pltpu.make_async_remote_copy(
            src_ref=fc.at[row, at, pl.ds(col, REGION_VALUES)],
            dst_ref=rbuf.at[i, pl.ds(me * members + c * per_chunk, per_chunk), :],
            send_sem=asend.at[c, d - 1, i],
            recv_sem=arecv.at[c, d - 1, i],
            device_id=(peer, strip),
            device_id_type=MESH,
        )

    tiles = per_chunk // TILE
    for c in range(chunks):

        def body(t, carry, c=c):
            march(c * tiles + t)
            return carry

        lax.fori_loop(0, tiles, body, 0)
        for i in range(groups):
            for d in range(1, n_mem):
                out_copy(c, d, i).start()

    own = pl.ds(pl.multiple_of(me * members, TILE), members)
    for i in range(groups):
        row, col = place(me, i)
        rbuf[i, own, :] = fc[row, :, pl.ds(col, REGION_VALUES)]

    eye = (
        lax.broadcasted_iota(jnp.int32, (obs, obs), 0)
        == lax.broadcasted_iota(jnp.int32, (obs, obs), 1)
    ).astype(f32)
    spread_dof = float(total - 1)

    def prepare(i):
        for c in range(chunks):
            for d in range(1, n_mem):
                out_copy(c, d, i).wait_recv()
        values = rbuf[i]
        mean = jnp.sum(values, axis=0, keepdims=True) * (1.0 / total)
        spread = values - mean
        rbuf[i] = spread
        s_hi, s_lo = split(spread)
        onehot = (
            lax.broadcasted_iota(jnp.int32, (REGION_VALUES, obs), 0) == index_ref[i : i + 1, :]
        ).astype(f32).astype(bf16)
        both = dot(jnp.concatenate([s_hi, s_lo], axis=0), onehot)
        obs_spread = both[:total] + both[total:]
        m_hi = mean.astype(bf16)
        rest = mean - m_hi.astype(f32)
        m_mid = rest.astype(bf16)
        m_lo = (rest - m_mid.astype(f32)).astype(bf16)
        mean_rows = [jnp.broadcast_to(p, (16, REGION_VALUES)) for p in (m_hi, m_mid, m_lo)]
        picked = dot(jnp.concatenate(mean_rows, axis=0), onehot)
        obs_mean = picked[0:1] + picked[16:17] + picked[32:33]
        slots = lax.broadcasted_iota(jnp.int32, (1, obs), 1)
        weight = jnp.where(slots < count_ref[i], prec_ref[i : i + 1, :], 0.0)
        root = jnp.sqrt(weight)
        u_row = root * (value_ref[i : i + 1, :] - obs_mean)
        u_col = jnp.sum(eye * u_row, axis=1, keepdims=True)
        bt = obs_spread * root
        b = bt.T
        bt_wide = wide_lhs(bt)
        bt_ref[i] = bt_wide
        b_hi, b_lo = split(b)
        b_tall = jnp.concatenate([b_hi, b_lo], axis=0)
        k4 = dot(b_tall, bt_wide)
        gram = (k4[:obs, :obs] + k4[obs:, obs:]) + (k4[:obs, obs:] + k4[obs:, :obs])
        e2 = dot(b_tall, s_hi)
        e_ref[i] = e2[:obs] + e2[obs:] + dot(b_hi, s_lo)
        return mean, gram, u_col

    prepared = [prepare(i) for i in range(groups)]

    def invert(gram):
        squares = jnp.sum(jnp.sum(gram * gram, axis=0, keepdims=True), axis=1, keepdims=True)
        scale = spread_dof + jnp.sqrt(squares)
        inv = 1.0 / scale
        a0 = spread_dof * inv
        left = a0 * eye + inv * gram
        right = 1.5 * eye - 0.5 * left
        r0 = 1.5 - 0.5 * a0
        l0 = a0 * r0
        rq = None
        rq_scalar = -0.5 * inv
        (left,) = small_dot([left], right)
        for it in range(1, NS_ITERS):
            if rq is None:
                (product,) = small_dot([right], left)
                lq = inv * right + (a0 * rq_scalar) * eye
                pq = rq_scalar * left + r0 * lq
            else:
                product, rq_left = small_dot([right, rq], left)
                lq = inv * right + a0 * rq
                pq = rq_left + r0 * lq
            corr = 1.5 * eye - 0.5 * product
            cq = -0.5 * pq
            c0 = 1.5 - 0.5 * r0 * l0
            last = it == NS_ITERS - 1
            if rq is None:
                rq = rq_scalar * corr + r0 * cq
                left, right = small_dot([left, right], corr)
            elif last:
                right, moved = small_dot([right, rq], corr)
                rq = moved + r0 * cq
            else:
                left, right, moved = small_dot([left, right, rq], corr)
                rq = moved + r0 * cq
            r0, l0 = r0 * c0, l0 * c0
        return scale, right, r0, rq

    inverted = [invert(gram) for _, gram, _ in prepared]

    def back_copy(d, i):
        peer = lax.rem(me + d, n_mem)
        row, col = place(me, i)
        return pltpu.make_async_remote_copy(
            src_ref=ana.at[i, pl.ds(pl.multiple_of(peer * members, TILE), members), :],
            dst_ref=out_ref.at[row, :, pl.ds(col, REGION_VALUES)],
            send_sem=bsend.at[d - 1, i],
            recv_sem=brecv.at[d - 1, i],
            device_id=(peer, strip),
            device_id_type=MESH,
        )

    for i in range(groups):
        mean, _, u_col = prepared[i]
        scale, right, r0, rq = inverted[i]
        amp = math.sqrt(spread_dof) / jnp.sqrt(scale)
        e = e_ref[i]
        e_hi, e_lo = split(e)
        rq_wide = wide_lhs(amp * rq)
        z = dot(rq_wide, jnp.concatenate([e_hi, e_hi], axis=0)) + dot(
            rq_wide, jnp.concatenate([e_lo, e_lo], axis=0)
        )
        w1 = jnp.sum(u_col * right, axis=0, keepdims=True)
        w2 = jnp.sum(right * w1, axis=1, keepdims=True) / scale
        shift = mean + jnp.sum(w2 * e, axis=0, keepdims=True)
        z_hi, z_lo = split(z)
        bt_wide = bt_ref[i]
        moved = dot(bt_wide, jnp.concatenate([z_hi, z_hi], axis=0)) + dot(
            bt_wide, jnp.concatenate([z_lo, z_lo], axis=0)
        )
        ana[i] = moved + (amp * r0) * rbuf[i] + shift
        for d in range(1, n_mem):
            back_copy(d, i).start()
        row, col = place(me, i)
        out_ref[row, :, pl.ds(col, REGION_VALUES)] = ana[i, own, :]

    for side in range(2):

        @pl.when(sends[side])
        def _(side=side):
            halo_copy(side).wait_send()

    for c in range(chunks):
        for i in range(groups):
            for d in range(1, n_mem):
                out_copy(c, d, i).wait_send()
    for i in range(groups):
        for d in range(1, n_mem):
            back_copy(d, i).wait()


def local(n_mem, n_strip, ensemble, forcing, obs_index, obs_count, obs_value, obs_precision):
    members, rows, lon = ensemble.shape
    groups, obs = obs_index.shape
    total = members * n_mem
    chunks = max(1, members // (2 * TILE))
    x = jnp.concatenate(
        [
            jnp.transpose(ensemble, (1, 0, 2)),
            jnp.broadcast_to(forcing[:, None, :], (rows, TILE, lon)),
        ],
        axis=1,
    )
    vmem = pl.BlockSpec(memory_space=pltpu.VMEM)
    dma = pltpu.SemaphoreType.DMA
    out = pl.pallas_call(
        functools.partial(kernel, n_mem, n_strip, members),
        out_shape=jax.ShapeDtypeStruct((rows, members, lon), f32),
        in_specs=[pl.BlockSpec(memory_space=pltpu.SMEM)] + [vmem] * 4,
        out_specs=vmem,
        scratch_shapes=[
            pltpu.VMEM((2, STEPS, members + TILE, lon), f32),
            pltpu.VMEM((rows, members, lon), f32),
            pltpu.VMEM((groups, total, REGION_VALUES), f32),
            pltpu.VMEM((groups, total, REGION_VALUES), f32),
            pltpu.VMEM((groups, total, 2 * obs), bf16),
            pltpu.VMEM((groups, obs, REGION_VALUES), f32),
            dma((2,)),
            dma((2,)),
            dma((chunks, n_mem - 1, groups)),
            dma((chunks, n_mem - 1, groups)),
            dma((n_mem - 1, groups)),
            dma((n_mem - 1, groups)),
        ],
        compiler_params=pltpu.CompilerParams(
            collective_id=0, has_side_effects=True, vmem_limit_bytes=48 * 1024 * 1024
        ),
    )(obs_count, x, obs_index, obs_value, obs_precision)
    return jnp.transpose(out, (1, 0, 2))


def solution(mesh):
    placed = (
        P("mem", "strip", None),
        P("strip", None),
        P(("strip", "mem"), None),
        P(("strip", "mem")),
        P(("strip", "mem"), None),
        P(("strip", "mem"), None),
    )
    return jax.shard_map(
        functools.partial(local, mesh.shape["mem"], mesh.shape["strip"]),
        mesh=mesh,
        in_specs=placed,
        out_specs=P("mem", "strip", None),
        check_vma=False,
    )
```

time: 59 us -> 31.8 us (0.54); the launches traced: 57.9 us -> 31.6 us
  Pallas kernels: 0 us -> 27.8 us
  waiting for transfers between devices: 13.1 us -> 0 us
  matrix products: 10.8 us -> 0 us
  blocking collectives: 10.4 us -> 0 us
  starting transfers between devices: 9.47 us -> 0 us
  other arithmetic: 5.56 us -> 0.05 us
  local copies, waits for them, and re-layouts: 8.07 us -> 3.64 us
    pallas_call x0 -> x1, Pallas kernels: none -> 27.8 us  [local(): pl.pallas_call(functools.partial(kernel, n_mem, n_strip, members), out_sh...]
    dot_general x18 -> x0, matrix products: 10.8 us -> none  [the longest x4 2.7 us: analyze(): jnp.einsum('rij,rjk->rik', right_iterate, left_iterate, precision=highest)]
    all_to_all x1 -> x0, blocking collectives: 10.4 us -> none  [local(): lax.all_to_all(analysis, 'mem', split_axis=0, concat_axis=1, tiled=True)]
    all_to_all x1 -> x0, waiting for transfers between devices: 7.39 us -> none  [local(): lax.all_to_all(flat_state, 'mem', split_axis=1, concat_axis=0, tiled=True)]
    ppermute x2 -> x0, starting transfers between devices: 5.82 us -> none  [the longest x1 3.9 us: padded(): lax.ppermute(lax.slice_in_dim(block, block.shape[dim] - width, None, axis...]
    ppermute x2 -> x0, waiting for transfers between devices: 5.7 us -> none  [the longest x1 4.35 us: padded(): lax.ppermute(lax.slice_in_dim(block, 0, width, axis=dim), axis, backward)]
    mul x6 -> x0, other arithmetic: 3.78 us -> none  [the longest x4 3.67 us: local(): advanced * inside[sweep_index + 1:sweep_index + 1 + rows_next][None, :, N...]
    slice x22 -> x0, local copies, waits for them, and re-layouts: 3.71 us -> none  [the longest x8 2.16 us: march_forward(): jnp.roll(center, 1, 2)]
  transfers between devices with their start and end apart: 3 -> 0, of which waited for: 3 -> 0; matrix products, arithmetic and copies ran while one was open for 1% -> 0% of each run, Pallas kernels for 0% -> 0%
where the time goes in v1:
time: 31.8 us; the launch traced here: 31.6 us
  Pallas kernels  27.8 us (87%)
  local copies, waits for them, and re-layouts  3.64 us (11%)
    pallas_call x1, Pallas kernels, local(): pl.pallas_call(functools.partial(kernel, n_mem, n_strip, members), out_sh...  27.8 us
    unnamed x9, local copies, waits for them, and re-layouts  1.84 us
    transpose x1, local copies, waits for them, and re-layouts, local(): return jnp.transpose(out, (1, 0, 2))  1.1 us
    broadcast_in_dim x1, local copies, waits for them, and re-layouts, local(): jnp.broadcast_to(forcing[:, None, :], (rows, TILE, lon))  0.7 us

profile of v1, /device:TPU:17, one launch (start us, length us, event | category | flops | bytes accessed | tf_op | source)
XLA Modules:
  0.0 31.6 jit_solution(2279489926048031795)
XLA Ops:
  0.0 0.7 %broadcast_in_dim.2 = f32[8,8,256]{2,1,0:T(8,128)S(1)} broadcast(f32[8,256]{1,0:T(8,128)} %param.7), dimensions={0,2} | broadcast | bytes 73728 | tf_op jit(solution)/shard_map/broadcast_in_dim | solution.py:344
  0.7 1.2 %copy.10 = f32[64,8,256]{2,0,1:T(8,128)S(1)} copy(f32[64,8,256]{2,1,0:T(8,128)} %param.6) | data formatting | bytes 1048576 | tf_op args[0]
  1.9 0.0 copy-start
  1.9 0.0 copy-start.1
  1.9 0.0 copy-start.2
  2.0 0.0 copy-start.3
  2.0 0.6 %copy-done = s32[2,128]{1,0:T(2,128)S(1)} copy-done((s32[2,128]{1,0:T(2,128)S(1)}, s32[2,128]{1,0:T(2,128)}, u32[]{:S(2)}) %copy-start) | copy-done | bytes 1048
  2.6 0.0 copy-done.1
  2.6 0.0 copy-done.2
  2.6 0.0 copy-done.3
  2.6 27.8 %shard_map.64 = f32[8,64,256]{2,1,0:T(8,128)S(1)} custom-call(s32[2]{0:T(128)S(1)} %copy-done.3, f32[8,72,256]{2,1,0:T(8,128)S(1)} %pad_maximum_fusion.x_ref, s32[2,128]{1,0:T(2,128)S(1)} %copy-done, f32[2,128]{1,0:T(2,128)S(1)} %copy-done.1, f32[2,128]{1,0:T(2,128)S(1)} %copy-done.2), custom_call_target="tpu_custom_call" | custom-call | tf_op jit(solution)/shard_map/pallas_call | solution.py:350
  30.5 1.1 %copy.8 = f32[64,8,256]{2,1,0:T(8,128)} copy(f32[64,8,256]{2,0,1:T(8,128)S(1)} %bitcast.4) | data formatting | bytes 1048576 | tf_op jit(solution)/shard_map/transpose | solution.py:373
  (1 shorter events, 0.0 us)
Async XLA Ops:
  1.9 0.7 %copy-start = (s32[2,128]{1,0:T(2,128)S(1)}, s32[2,128]{1,0:T(2,128)}, u32[]{:S(2)}) copy-start(s32[2,128]{1,0:T(2,128)} %index_ref.1) | copy-start | bytes 3076
  1.9 0.7 %copy-start.1 = (f32[2,128]{1,0:T(2,128)S(1)}, f32[2,128]{1,0:T(2,128)}, u32[]{:S(2)}) copy-start(f32[2,128]{1,0:T(2,128)} %value_ref.1) | copy-start | bytes 3076
  1.9 0.7 %copy-start.2 = (f32[2,128]{1,0:T(2,128)S(1)}, f32[2,128]{1,0:T(2,128)}, u32[]{:S(2)}) copy-start(f32[2,128]{1,0:T(2,128)} %prec_ref.1) | copy-start | bytes 3076
  2.0 0.7 %copy-start.3 = (s32[2]{0:T(128)S(1)}, s32[2]{0:T(128)}, u32[]{:S(2)}) copy-start(s32[2]{0:T(128)} %count_ref.1) | copy-start | bytes 28

commit v2 on v1

--- a/solution.py
+++ b/solution.py
@@ -12,6 +12,7 @@
 NS_ITERS = 4
 REGION_VALUES = 256
 TILE = 8
+LANES = 128
 
 step_size = 0.05
 coupling = 0.4
@@ -52,13 +53,21 @@
     n_mem,
     n_strip,
     members,
+    ens_hbm,
+    forcing_hbm,
+    index_hbm,
+    count_hbm,
+    value_hbm,
+    prec_hbm,
+    out_ref,
     count_ref,
-    x_ref,
     index_ref,
     value_ref,
     prec_ref,
-    out_ref,
+    x_ref,
     halo,
+    forcing_ref,
+    pushed,
     fc,
     rbuf,
     ana,
@@ -70,8 +79,12 @@
     arecv,
     bsend,
     brecv,
+    fsend,
+    frecv,
+    lsem,
 ):
-    rows, padded_members, lon = x_ref.shape
+    lanes, _, rows, _ = x_ref.shape
+    lon = lanes * LANES
     groups, obs = index_ref.shape
     chunks = asend.shape[0]
     per_chunk = members // chunks
@@ -85,6 +98,18 @@
         flat = (owner * groups + i) * REGION_VALUES
         return flat // lon, pl.multiple_of(flat % lon, REGION_VALUES)
 
+    moves = [(ens_hbm.at[:, :, pl.ds(h * LANES, LANES)], x_ref.at[h]) for h in range(lanes)]
+    moves += [
+        (forcing_hbm, forcing_ref.at[1]),
+        (index_hbm, index_ref),
+        (value_hbm, value_ref),
+        (prec_hbm, prec_ref),
+        (count_hbm, count_ref),
+    ]
+    loads = [pltpu.make_async_copy(*move, lsem.at[k]) for k, move in enumerate(moves)]
+    for load in loads:
+        load.start()
+
     barrier = pltpu.get_barrier_semaphore()
     for d in range(1, n_mem):
         pl.semaphore_signal(
@@ -103,15 +128,38 @@
         barrier, n_mem - 1 + jnp.where(has_low, 1, 0) + jnp.where(has_high, 1, 0)
     )
 
-    def halo_copy(side):
+    def halo_side(side):
+        at = pl.ds(rows - STEPS if side == 0 else 0, STEPS)
+        return at, (me, strip + 1 if side == 0 else strip - 1)
+
+    def halo_copies(side, c):
+        at, target = halo_side(side)
+        part = pl.ds(c * per_chunk, per_chunk)
+        return [
+            pltpu.make_async_remote_copy(
+                src_ref=ens_hbm.at[part, at, pl.ds(h * LANES, LANES)],
+                dst_ref=halo.at[h, part, at, :],
+                send_sem=hsend.at[side, c, h],
+                recv_sem=hrecv.at[side, c, h],
+                device_id=target,
+                device_id_type=MESH,
+            )
+            for h in range(lanes)
+        ]
+
+    def forcing_copy(side):
         return pltpu.make_async_remote_copy(
-            src_ref=x_ref.at[pl.ds(rows - STEPS if side == 0 else 0, STEPS)],
-            dst_ref=halo.at[side],
-            send_sem=hsend.at[side],
-            recv_sem=hrecv.at[side],
-            device_id=(me, strip + 1 if side == 0 else strip - 1),
+            src_ref=forcing_hbm,
+            dst_ref=forcing_ref.at[2 * side],
+            send_sem=fsend.at[side],
+            recv_sem=frecv.at[side],
+            device_id=halo_side(side)[1],
             device_id_type=MESH,
         )
+
+    def all_halo_copies(side):
+        parts = [copy for c in range(chunks) for copy in halo_copies(side, c)]
+        return [forcing_copy(side)] + parts
 
     sends = (has_high, has_low)
     receives = (has_low, has_high)
@@ -119,32 +167,44 @@
 
         @pl.when(sends[side])
         def _(side=side):
-            halo_copy(side).start()
+            for copy in all_halo_copies(side):
+                copy.start()
 
         @pl.when(jnp.logical_not(receives[side]))
         def _(side=side):
-            halo[side] = jnp.zeros(halo.shape[1:], f32)
-
+            at, _ = halo_side(side)
+            halo[:, :, at, :] = jnp.zeros((lanes, members, STEPS, LANES), f32)
+            forcing_ref[2 * side] = jnp.zeros((rows, lon), f32)
+
+    for load in loads:
+        load.wait()
     for side in range(2):
 
         @pl.when(receives[side])
         def _(side=side):
-            halo_copy(side).wait_recv()
+            forcing_copy(side).wait_recv()
 
     low_in = jnp.where(has_low, 1.0, 0.0).astype(f32)
     high_in = jnp.where(has_high, 1.0, 0.0).astype(f32)
 
-    def stacked(r, at):
-        if r < STEPS:
-            return halo[0, r, at, :]
-        if r < STEPS + rows:
-            return x_ref[r - STEPS, at, :]
-        return halo[1, r - STEPS - rows, at, :]
+    x_flat = x_ref.reshape(lanes * members * rows, LANES)
+    halo_flat = halo.reshape(lanes * members * rows, LANES)
+    for r in range(1, rows + 2 * STEPS - 1):
+        side, row = divmod(r - STEPS + rows, rows)
+        pushed[r] = jnp.broadcast_to(step_size * forcing_ref[side, row : row + 1, :], (TILE, lon))
 
     def march(tile):
         at = pl.ds(pl.multiple_of(tile * TILE, TILE), TILE)
-        force_at = pl.ds(members, TILE)
-        state = [stacked(r, at) for r in range(rows + 2 * STEPS)]
+
+        def row_of(r):
+            side, row = divmod(r - STEPS + rows, rows)
+            source = x_flat if side == 1 else halo_flat
+            starts = [(h * members + tile * TILE) * rows + row for h in range(lanes)]
+            return jnp.concatenate(
+                [source[pl.ds(start, TILE, stride=rows), :] for start in starts], axis=1
+            )
+
+        state = [row_of(r) for r in range(rows + 2 * STEPS)]
         first = 0
         for _ in range(STEPS):
             following = []
@@ -154,7 +214,7 @@
                 advection = (pltpu.roll(u, lon - 1, 1) - pltpu.roll(u, 2, 1)) * pltpu.roll(u, 1, 1)
                 new = (
                     (1.0 - step_size - 2.0 * coupling) * u
-                    + step_size * (advection + stacked(r, force_at))
+                    + (step_size * advection + pushed[r])
                     + coupling * (state[k - 1] + state[k + 1])
                 )
                 if r < STEPS:
@@ -182,13 +242,22 @@
 
     tiles = per_chunk // TILE
     for c in range(chunks):
+        for side in range(2):
+
+            @pl.when(receives[side])
+            def _(side=side, c=c):
+                for copy in halo_copies(side, c):
+                    copy.wait_recv()
 
         def body(t, carry, c=c):
             march(c * tiles + t)
             return carry
 
         lax.fori_loop(0, tiles, body, 0)
-        for i in range(groups):
+        for d in range(1, n_mem):
+            out_copy(c, d, 0).start()
+    for i in range(1, groups):
+        for c in range(chunks):
             for d in range(1, n_mem):
                 out_copy(c, d, i).start()
 
@@ -225,7 +294,7 @@
         picked = dot(jnp.concatenate(mean_rows, axis=0), onehot)
         obs_mean = picked[0:1] + picked[16:17] + picked[32:33]
         slots = lax.broadcasted_iota(jnp.int32, (1, obs), 1)
-        weight = jnp.where(slots < count_ref[i], prec_ref[i : i + 1, :], 0.0)
+        weight = jnp.where(slots < count_ref[0:1, i : i + 1], prec_ref[i : i + 1, :], 0.0)
         root = jnp.sqrt(weight)
         u_row = root * (value_ref[i : i + 1, :] - obs_mean)
         u_col = jnp.sum(eye * u_row, axis=1, keepdims=True)
@@ -241,7 +310,6 @@
         e_ref[i] = e2[:obs] + e2[obs:] + dot(b_hi, s_lo)
         return mean, gram, u_col
 
-    prepared = [prepare(i) for i in range(groups)]
 
     def invert(gram):
         squares = jnp.sum(jnp.sum(gram * gram, axis=0, keepdims=True), axis=1, keepdims=True)
@@ -280,7 +348,6 @@
             r0, l0 = r0 * c0, l0 * c0
         return scale, right, r0, rq
 
-    inverted = [invert(gram) for _, gram, _ in prepared]
 
     def back_copy(d, i):
         peer = lax.rem(me + d, n_mem)
@@ -295,8 +362,8 @@
         )
 
     for i in range(groups):
-        mean, _, u_col = prepared[i]
-        scale, right, r0, rq = inverted[i]
+        mean, gram, u_col = prepare(i)
+        scale, right, r0, rq = invert(gram)
         amp = math.sqrt(spread_dof) / jnp.sqrt(scale)
         e = e_ref[i]
         e_hi, e_lo = split(e)
@@ -322,7 +389,8 @@
 
         @pl.when(sends[side])
         def _(side=side):
-            halo_copy(side).wait_send()
+            for copy in all_halo_copies(side):
+                copy.wait_send()
 
     for c in range(chunks):
         for i in range(groups):
@@ -337,39 +405,43 @@
     members, rows, lon = ensemble.shape
     groups, obs = obs_index.shape
     total = members * n_mem
+    lanes = lon // LANES
     chunks = max(1, members // (2 * TILE))
-    x = jnp.concatenate(
-        [
-            jnp.transpose(ensemble, (1, 0, 2)),
-            jnp.broadcast_to(forcing[:, None, :], (rows, TILE, lon)),
-        ],
-        axis=1,
-    )
     vmem = pl.BlockSpec(memory_space=pltpu.VMEM)
     dma = pltpu.SemaphoreType.DMA
     out = pl.pallas_call(
         functools.partial(kernel, n_mem, n_strip, members),
         out_shape=jax.ShapeDtypeStruct((rows, members, lon), f32),
-        in_specs=[pl.BlockSpec(memory_space=pltpu.SMEM)] + [vmem] * 4,
+        in_specs=[pl.BlockSpec(memory_space=pl.ANY)] * 6,
         out_specs=vmem,
         scratch_shapes=[
-            pltpu.VMEM((2, STEPS, members + TILE, lon), f32),
+            pltpu.VMEM((1, groups), jnp.int32),
+            pltpu.VMEM((groups, obs), jnp.int32),
+            pltpu.VMEM((groups, obs), f32),
+            pltpu.VMEM((groups, obs), f32),
+            pltpu.VMEM((lanes, members, rows, LANES), f32),
+            pltpu.VMEM((lanes, members, rows, LANES), f32),
+            pltpu.VMEM((3, rows, lon), f32),
+            pltpu.VMEM((rows + 2 * STEPS, TILE, lon), f32),
             pltpu.VMEM((rows, members, lon), f32),
             pltpu.VMEM((groups, total, REGION_VALUES), f32),
             pltpu.VMEM((groups, total, REGION_VALUES), f32),
             pltpu.VMEM((groups, total, 2 * obs), bf16),
             pltpu.VMEM((groups, obs, REGION_VALUES), f32),
-            dma((2,)),
-            dma((2,)),
+            dma((2, chunks, lanes)),
+            dma((2, chunks, lanes)),
             dma((chunks, n_mem - 1, groups)),
             dma((chunks, n_mem - 1, groups)),
             dma((n_mem - 1, groups)),
             dma((n_mem - 1, groups)),
+            dma((2,)),
+            dma((2,)),
+            dma((lanes + 5,)),
         ],
         compiler_params=pltpu.CompilerParams(
-            collective_id=0, has_side_effects=True, vmem_limit_bytes=48 * 1024 * 1024
+            collective_id=0, has_side_effects=True, vmem_limit_bytes=67043328
         ),
-    )(obs_count, x, obs_index, obs_value, obs_precision)
+    )(ensemble, forcing, obs_index, obs_count[None], obs_value, obs_precision)
     return jnp.transpose(out, (1, 0, 2))
 
 

time: 31.8 us -> 26.3 us (0.83)
  Pallas kernels: 27.8 us -> 23.9 us
  local copies, waits for them, and re-layouts: 3.64 us -> 2.14 us
    pallas_call x1, Pallas kernels: 27.8 us -> 23.9 us  [local(): pl.pallas_call(functools.partial(kernel, n_mem, n_strip, members), out_sh...]
    unnamed x9 -> x0, local copies, waits for them, and re-layouts: 1.84 us -> none
    transpose x1, local copies, waits for them, and re-layouts: 1.1 us -> 2.14 us  [local(): return jnp.transpose(out, (1, 0, 2))]
    broadcast_in_dim x1 -> x0, local copies, waits for them, and re-layouts: 0.7 us -> none  [local(): jnp.broadcast_to(forcing[:, None, :], (rows, TILE, lon))]
where the time goes in v2:
time: 26.3 us; the launch traced here: 26.1 us
  Pallas kernels  23.9 us (91%)
  local copies, waits for them, and re-layouts  2.14 us (8%)
    pallas_call x1, Pallas kernels, local(): pl.pallas_call(functools.partial(kernel, n_mem, n_strip, members), out_sh...  23.9 us
    transpose x1, local copies, waits for them, and re-layouts, local(): return jnp.transpose(out, (1, 0, 2))  2.14 us

profile of v2, /device:TPU:17, one launch (start us, length us, event | category | flops | bytes accessed | tf_op | source)
XLA Modules:
  0.0 26.1 jit_solution(12015019235273838968)
XLA Ops:
  0.0 23.9 %shard_map.64 = f32[8,64,256]{2,1,0:T(8,128)} custom-call(f32[64,8,256]{2,1,0:T(8,128)} %ens_hbm.1, f32[8,256]{1,0:T(8,128)} %forcing_hbm.1, s32[2,128]{1,0:T(2,128)} %index_hbm.1, s32[1,2]{1,0:T(1,128)} %bitcast.3, f32[2,128]{1,0:T(2,128)} %value_hbm.1, f32[2,128]{1,0:T(2,128)} %prec_hbm.1), custom_call_target="tpu_custom_call" | custom-call | tf_op jit(solution)/shard_map/pallas_call | solution.py:412
  24.0 2.1 %copy.7 = f32[64,8,256]{2,1,0:T(8,128)} copy(f32[64,8,256]{2,0,1:T(8,128)} %bitcast.2) | data formatting | bytes 1048576 | tf_op jit(solution)/shard_map/transpose | solution.py:445

commit v3 on v2

--- a/solution.py
+++ b/solution.py
@@ -68,6 +68,7 @@
     halo,
     forcing_ref,
     pushed,
+    mid,
     fc,
     rbuf,
     ana,
@@ -178,54 +179,84 @@
 
     for load in loads:
         load.wait()
-    for side in range(2):
-
-        @pl.when(receives[side])
-        def _(side=side):
-            forcing_copy(side).wait_recv()
-
     low_in = jnp.where(has_low, 1.0, 0.0).astype(f32)
     high_in = jnp.where(has_high, 1.0, 0.0).astype(f32)
 
     x_flat = x_ref.reshape(lanes * members * rows, LANES)
     halo_flat = halo.reshape(lanes * members * rows, LANES)
-    for r in range(1, rows + 2 * STEPS - 1):
-        side, row = divmod(r - STEPS + rows, rows)
-        pushed[r] = jnp.broadcast_to(step_size * forcing_ref[side, row : row + 1, :], (TILE, lon))
-
-    def march(tile):
-        at = pl.ds(pl.multiple_of(tile * TILE, TILE), TILE)
-
-        def row_of(r):
+    def push(ext_rows):
+        for r in ext_rows:
             side, row = divmod(r - STEPS + rows, rows)
-            source = x_flat if side == 1 else halo_flat
-            starts = [(h * members + tile * TILE) * rows + row for h in range(lanes)]
-            return jnp.concatenate(
-                [source[pl.ds(start, TILE, stride=rows), :] for start in starts], axis=1
+            pushed[r] = jnp.broadcast_to(
+                step_size * forcing_ref[side, row : row + 1, :], (TILE, lon)
             )
 
-        state = [row_of(r) for r in range(rows + 2 * STEPS)]
-        first = 0
-        for _ in range(STEPS):
-            following = []
-            for k in range(1, len(state) - 1):
-                r = first + k
-                u = state[k]
-                advection = (pltpu.roll(u, lon - 1, 1) - pltpu.roll(u, 2, 1)) * pltpu.roll(u, 1, 1)
-                new = (
-                    (1.0 - step_size - 2.0 * coupling) * u
-                    + (step_size * advection + pushed[r])
-                    + coupling * (state[k - 1] + state[k + 1])
-                )
-                if r < STEPS:
-                    new = new * low_in
-                elif r >= STEPS + rows:
-                    new = new * high_in
-                following.append(new)
-            state = following
-            first += 1
+    def inner(step, row):
+        return 0 < step < STEPS and step <= row < rows - step
+
+    def kept(step, row):
+        return inner(step, row) and not inner(step + 1, row - 1) or (
+            inner(step, row) and not (inner(step + 1, row) and inner(step + 1, row + 1))
+        )
+
+    slots = [(s, r) for s in range(1, STEPS) for r in range(rows) if kept(s, r)]
+
+    def advance(above, u, below, row):
+        advection = (pltpu.roll(u, lon - 1, 1) - pltpu.roll(u, 2, 1)) * pltpu.roll(u, 1, 1)
+        new = (
+            (1.0 - step_size - 2.0 * coupling) * u
+            + (step_size * advection + pushed[row + STEPS])
+            + coupling * (above + below)
+        )
+        if row < 0:
+            new = new * low_in
+        elif row >= rows:
+            new = new * high_in
+        return new
+
+    def row_of(tile, row):
+        side, row = divmod(row + rows, rows)
+        source = x_flat if side == 1 else halo_flat
+        starts = [(h * members + tile * TILE) * rows + row for h in range(lanes)]
+        return jnp.concatenate(
+            [source[pl.ds(start, TILE, stride=rows), :] for start in starts], axis=1
+        )
+
+    def tile_at(tile):
+        return pl.ds(pl.multiple_of(tile * TILE, TILE), TILE)
+
+    def march_inner(tile):
+        current = {r: row_of(tile, r) for r in range(rows)}
+        for step in range(1, STEPS):
+            current = {
+                r: advance(current[r - 1], current[r], current[r + 1], r)
+                for r in range(rows)
+                if inner(step, r)
+            }
+            for r in current:
+                if (step, r) in slots:
+                    mid[slots.index((step, r)), tile_at(tile), :] = current[r]
+
+    def march_outer(tile):
+        current = {}
+
+        def value(step, r):
+            if r not in current:
+                if step == 0:
+                    current[r] = row_of(tile, r)
+                else:
+                    current[r] = mid[slots.index((step, r)), tile_at(tile), :]
+            return current[r]
+
+        for step in range(1, STEPS + 1):
+            reach = STEPS - step
+            current = {
+                r: advance(*(value(step - 1, r + k) for k in (-1, 0, 1)), r)
+                for r in range(-reach, rows + reach)
+                if not inner(step, r)
+            }
         for r in range(rows):
-            fc[r, at, :] = state[r]
+            fc[r, tile_at(tile), :] = current[r]
 
     def out_copy(c, d, i):
         peer = lax.rem(me + d, n_mem)
@@ -240,6 +271,21 @@
             device_id_type=MESH,
         )
 
+    push(range(STEPS, STEPS + rows))
+
+    def inner_body(t, carry):
+        march_inner(t)
+        return carry
+
+    lax.fori_loop(0, members // TILE, inner_body, 0)
+    for side in range(2):
+
+        @pl.when(receives[side])
+        def _(side=side):
+            forcing_copy(side).wait_recv()
+    push(range(1, STEPS))
+    push(range(STEPS + rows, rows + 2 * STEPS - 1))
+
     tiles = per_chunk // TILE
     for c in range(chunks):
         for side in range(2):
@@ -250,10 +296,10 @@
                     copy.wait_recv()
 
         def body(t, carry, c=c):
-            march(c * tiles + t)
+            march_outer(c * tiles + t)
             return carry
 
-        lax.fori_loop(0, tiles, body, 0)
+        lax.fori_loop(0, tiles, body, 0, unroll=True)
         for d in range(1, n_mem):
             out_copy(c, d, 0).start()
     for i in range(1, groups):
@@ -301,7 +347,7 @@
         bt = obs_spread * root
         b = bt.T
         bt_wide = wide_lhs(bt)
-        bt_ref[i] = bt_wide
+        bt_ref[i] = bt
         b_hi, b_lo = split(b)
         b_tall = jnp.concatenate([b_hi, b_lo], axis=0)
         k4 = dot(b_tall, bt_wide)
@@ -375,15 +421,19 @@
         w2 = jnp.sum(right * w1, axis=1, keepdims=True) / scale
         shift = mean + jnp.sum(w2 * e, axis=0, keepdims=True)
         z_hi, z_lo = split(z)
-        bt_wide = bt_ref[i]
-        moved = dot(bt_wide, jnp.concatenate([z_hi, z_hi], axis=0)) + dot(
-            bt_wide, jnp.concatenate([z_lo, z_lo], axis=0)
-        )
-        ana[i] = moved + (amp * r0) * rbuf[i] + shift
-        for d in range(1, n_mem):
-            back_copy(d, i).start()
-        row, col = place(me, i)
-        out_ref[row, :, pl.ds(col, REGION_VALUES)] = ana[i, own, :]
+        z_high = jnp.concatenate([z_hi, z_hi], axis=0)
+        z_low = jnp.concatenate([z_lo, z_lo], axis=0)
+        for d in (*range(1, n_mem), 0):
+            at = pl.ds(pl.multiple_of(lax.rem(me + d, n_mem) * members, TILE), members)
+            bt_wide = wide_lhs(bt_ref[i, at, :])
+            moved = dot(bt_wide, z_high) + dot(bt_wide, z_low)
+            block = moved + (amp * r0) * rbuf[i, at, :] + shift
+            if d:
+                ana[i, at, :] = block
+                back_copy(d, i).start()
+            else:
+                row, col = place(me, i)
+                out_ref[row, :, pl.ds(col, REGION_VALUES)] = block
 
     for side in range(2):
 
@@ -423,10 +473,11 @@
             pltpu.VMEM((lanes, members, rows, LANES), f32),
             pltpu.VMEM((3, rows, lon), f32),
             pltpu.VMEM((rows + 2 * STEPS, TILE, lon), f32),
+            pltpu.VMEM((STEPS * rows, members, lon), f32),
             pltpu.VMEM((rows, members, lon), f32),
             pltpu.VMEM((groups, total, REGION_VALUES), f32),
             pltpu.VMEM((groups, total, REGION_VALUES), f32),
-            pltpu.VMEM((groups, total, 2 * obs), bf16),
+            pltpu.VMEM((groups, total, obs), f32),
             pltpu.VMEM((groups, obs, REGION_VALUES), f32),
             dma((2, chunks, lanes)),
             dma((2, chunks, lanes)),
@@ -439,9 +490,9 @@
             dma((lanes + 5,)),
         ],
         compiler_params=pltpu.CompilerParams(
-            collective_id=0, has_side_effects=True, vmem_limit_bytes=67043328
+            collective_id=0, has_side_effects=True, vmem_limit_bytes=48 * 1024 * 1024
         ),
-    )(ensemble, forcing, obs_index, obs_count[None], obs_value, obs_precision)
+    )(*[pltpu.with_memory_space_constraint(a, pltpu.HBM) for a in (ensemble, forcing, obs_index, obs_count[None], obs_value, obs_precision)])
     return jnp.transpose(out, (1, 0, 2))
 
 

time: 26.3 us -> 23.9 us (0.909)
  Pallas kernels: 23.9 us -> 22.4 us
  local copies, waits for them, and re-layouts: 2.14 us -> 1.1 us
    pallas_call x1, Pallas kernels: 23.9 us -> 22.4 us  [local(): pl.pallas_call(functools.partial(kernel, n_mem, n_strip, members), out_sh...]
    transpose x1, local copies, waits for them, and re-layouts: 2.14 us -> 1.1 us  [local(): return jnp.transpose(out, (1, 0, 2))]
where the time goes in v3:
time: 23.9 us; the launch traced here: 23.5 us
  Pallas kernels  22.4 us (94%)
  local copies, waits for them, and re-layouts  1.1 us (5%)
    pallas_call x1, Pallas kernels, local(): pl.pallas_call(functools.partial(kernel, n_mem, n_strip, members), out_sh...  22.4 us
    transpose x1, local copies, waits for them, and re-layouts, local(): return jnp.transpose(out, (1, 0, 2))  1.1 us

profile of v3, /device:TPU:17, one launch (start us, length us, event | category | flops | bytes accessed | tf_op | source)
XLA Modules:
  0.0 23.5 jit_solution(6860486447430759262)
XLA Ops:
  0.0 22.4 %shard_map.64 = f32[8,64,256]{2,1,0:T(8,128)S(1)} custom-call(f32[64,8,256]{2,1,0:T(8,128)} %ens_hbm.1, f32[8,256]{1,0:T(8,128)} %forcing_hbm.1, s32[2,128]{1,0:T(2,128)} %index_hbm.1, s32[1,2]{1,0:T(1,128)} %bitcast.3, f32[2,128]{1,0:T(2,128)} %value_hbm.1, f32[2,128]{1,0:T(2,128)} %prec_hbm.1), custom_call_target="tpu_custom_call" | custom-call | tf_op jit(solution)/shard_map/pallas_call | solution.py:462
  22.4 1.1 %copy.7 = f32[64,8,256]{2,1,0:T(8,128)} copy(f32[64,8,256]{2,0,1:T(8,128)S(1)} %bitcast.2) | data formatting | bytes 1048576 | tf_op jit(solution)/shard_map/transpose | solution.py:496
